TPU v7x, 32 devices: a whole 2x2x4 slice. The times are simulated.
32 devices in a mesh: shot: 2 (over y), row: 4 (over x, core), freq: 4 (over z).
Axes of the slice: x: 2, y: 2, z: 4, core: 2. Of those that a mesh axis runs over, the one named last changes fastest.
Arguments:
- source_field: float32 [2, 8, 1024, 1024], P(None, ('shot', 'freq'), 'row'), parts along dimension 1, may hold values from -6 to 6
- receiver_field: float32 [2, 8, 1024, 1024], P(None, ('shot', 'freq'), 'row'), parts along dimension 1, may hold values from -6 to 6
- slowness: float32 [4, 1024, 1024], P('freq', 'row'), may hold values from 0.22 to 0.67
- owner: int32 [4], replicated, may hold values from 0 to 3, each once
- freq_index: int32 [8], P(('shot', 'freq')), parts along dimension 0, may hold values from 0 to 3, each once
Outputs:
- source_out: float32 [2, 8, 1024, 1024], P(None, ('shot', 'freq'), 'row'), parts along dimension 1
- receiver_out: float32 [2, 8, 1024, 1024], P(None, ('shot', 'freq'), 'row'), parts along dimension 1
- image: float32 [4, 1024, 1024], P('shot', 'row', 'freq'), parts along dimension 0
There are 2 independent parts, one for each index of `shot`. A program takes and returns all parts, laid end to end along the dimension named above; an argument that names none is the same for every part. Nothing has to cross between parts.
All inputs are finite; a program needn't handle non-finite values.
Results may differ from a plain program's by a relative error of at most 0.00022.
Values sent between devices are 32-bit elements; how exact they have to be, the bound alone decides.
A program may use at most 128 MiB of HBM per device.

v0:
```python
import math
import jax
import jax.numpy as jnp
from jax import lax
from jax.sharding import PartitionSpec as P

NZ = 2
dz_km = 0.01
dx_km = 0.0125
ref_slow = 0.5
base_hertz = 3.0
step_hertz = 4.0
taper = 0.5


def spread(value, axis, source):
    kept = jnp.where(lax.axis_index(axis) == source, value, 0).astype(value.dtype)
    return lax.psum(kept, axis)


def split_length(length):
    return length // 128


def angle_table(count_a, count_b, modulus, sign):
    left = jnp.arange(count_a, dtype=jnp.int32)[:, None]
    right = jnp.arange(count_b, dtype=jnp.int32)[None, :]
    turns = (left * right % modulus).astype(jnp.float32) * (2.0 * math.pi / modulus)
    return (jnp.cos(turns), sign * jnp.sin(turns))


def contract(form, left, right):
    return jnp.einsum(form, left, right, precision=lax.Precision.HIGHEST)


def transform_pair(real_part, imag_part, sign, last):
    length = real_part.shape[2] if last else real_part.shape[1]
    first = split_length(length)
    second = length // first
    cos_a, sin_a = angle_table(first, first, first, sign)
    cos_b, sin_b = angle_table(second, second, second, sign)
    twist_c, twist_s = angle_table(first, second, length, sign)
    if last:
        shape = (real_part.shape[0], real_part.shape[1], first, second)
        form_one = "fajb,jk->fakb"
        form_two = "fakb,bm->famk"
    else:
        shape = (real_part.shape[0], first, second, real_part.shape[2])
        form_one = "fjbq,jk->fkbq"
        form_two = "fkbq,bm->fmkq"
        twist_c = twist_c[:, :, None]
        twist_s = twist_s[:, :, None]
    x_re = real_part.reshape(shape)
    x_im = imag_part.reshape(shape)
    y_re = contract(form_one, x_re, cos_a) - contract(form_one, x_im, sin_a)
    y_im = contract(form_one, x_im, cos_a) + contract(form_one, x_re, sin_a)
    z_re = y_re * twist_c - y_im * twist_s
    z_im = y_im * twist_c + y_re * twist_s
    out_re = contract(form_two, z_re, cos_b) - contract(form_two, z_im, sin_b)
    out_im = contract(form_two, z_im, cos_b) + contract(form_two, z_re, sin_b)
    return (out_re.reshape(real_part.shape), out_im.reshape(real_part.shape))


def transform(block, sign, last):
    count = block.shape[0]
    freqs = block.shape[2]
    plane = block.shape[3:]
    real_part = block[:, 0].reshape((count * freqs,) + plane)
    imag_part = block[:, 1].reshape((count * freqs,) + plane)
    out_re, out_im = transform_pair(real_part, imag_part, sign, last)
    shape = (count, freqs) + plane
    return jnp.stack([out_re.reshape(shape), out_im.reshape(shape)], axis=1)


def wavenumbers(length, start, count):
    index = start + jnp.arange(count, dtype=jnp.int32)
    signed = jnp.where(index * 2 < length, index, index - length)
    return signed.astype(jnp.float32) * (2.0 * math.pi / (length * dx_km))


def rotate(block, cos_v, sin_v):
    real_part = block[:, 0]
    imag_part = block[:, 1]
    return jnp.stack(
        [real_part * cos_v - imag_part * sin_v, imag_part * cos_v + real_part * sin_v], axis=1
    )


def shift_phase(block, omega, kx_part, ky_part, total):
    square = kx_part[:, None] ** 2 + ky_part[None, :] ** 2
    kmax = math.pi / dx_km
    damp = jnp.exp(-taper * square / (kmax * kmax)) / total
    ws0 = omega[:, None, None] * ref_slow
    vertical = ws0 - 0.5 * square[None] / ws0
    cos_v = jnp.cos(dz_km * vertical) * damp
    sin_v = jnp.sin(dz_km * vertical) * damp
    return rotate(block, cos_v, sin_v)


def correct(block, slab, omega):
    theta = omega[:, None, None] * (slab[None] - ref_slow) * dz_km
    return rotate(block, jnp.cos(theta), jnp.sin(theta))


def image_term(block):
    return jnp.sum(block[0, 0] * block[1, 0] - block[0, 1] * block[1, 1], axis=0)


def body(source_field, receiver_field, slowness, owner, freq_index):
    rows = source_field.shape[2]
    width = source_field.shape[3]
    row_count = lax.axis_size("row")
    height = rows * row_count
    cols = width // row_count
    place = lax.axis_index("row")
    omega = 2.0 * math.pi * (base_hertz + step_hertz * freq_index.astype(jnp.float32))
    mirrored = jnp.stack([receiver_field[0], -receiver_field[1]])
    fields = jnp.stack([source_field, mirrored])
    kx_all = wavenumbers(height, 0, height)
    ky_own = wavenumbers(width, place * cols, cols)
    total = float(height * width)
    slab_dev = slowness.shape[0]
    images = []
    for depth in range(NZ):
        chosen = owner[depth]
        held = spread(slowness, "freq", chosen // slab_dev)
        slab = lax.dynamic_index_in_dim(held, chosen % slab_dev, 0, keepdims=False)
        fields = transform(fields, -1.0, True)
        fields = lax.all_to_all(fields, "row", split_axis=4, concat_axis=3, tiled=True)
        items = fields
        items = transform(items, -1.0, False)
        items = shift_phase(items, omega, kx_all, ky_own, total)
        fields = transform(items, 1.0, False)
        fields = lax.all_to_all(fields, "row", split_axis=3, concat_axis=4, tiled=True)
        fields = transform(fields, 1.0, True)
        fields = correct(fields, slab, omega)
        images.append(image_term(fields))
    parts = [lax.psum_scatter(term, "freq", scatter_dimension=1, tiled=True) for term in images]
    image = jnp.stack(parts)
    source_out = fields[0]
    receiver_out = jnp.stack([fields[1, 0], -fields[1, 1]])
    return (source_out, receiver_out, image)


def solution(mesh):
    in_specs = (
        P(None, ("shot", "freq"), "row", None),
        P(None, ("shot", "freq"), "row", None),
        P("freq", "row", None),
        P(),
        P(("shot", "freq")),
    )
    out_specs = (
        P(None, ("shot", "freq"), "row", None),
        P(None, ("shot", "freq"), "row", None),
        P("shot", "row", "freq"),
    )
    return jax.shard_map(body, mesh=mesh, in_specs=in_specs, out_specs=out_specs, check_vma=False)
```

profile of v0, /device:TPU:0, one launch (start us, length us, event | category | flops | bytes accessed | tf_op | source)
XLA Modules:
  0.0 596.2 jit_solution(643073891319918496)
XLA Ops:
  20.3 2.7 fusion.112
  32.7 5.4 copy.346
  38.1 4.9 all-to-all-start
  44.0 4.0 fusion.186
  48.1 43.7 %all-to-all-done = f32[2,2,1,256,1024]{3,0,2,1,4:T(2,128)} async-done(((f32[2,2,1,256,1024]{3,0,2,1,4:T(2,128)}), f32[2,2,1,256,1024]{3,0,2,1,4:T(2,128)}, u32[]{:S(2)}, u32[]{:S(2)}) %all-to-all-start) | async-done | bytes 4194336 | tf_op jit(solution)/shard_map/all_to_all | solution.py:129
  91.8 5.0 copy.347
  96.7 5.4 copy.348
  104.7 2.9 fusion.104
  107.6 2.9 fusion.102
  110.5 2.9 fusion.118
  113.4 3.8 subtract_bitcast_fusion.13
  122.4 2.6 subtract_bitcast_fusion.12
  126.3 2.6 add_bitcast_fusion.12
  131.0 2.9 fusion.88
  133.9 2.9 fusion.86
  136.8 3.0 fusion.124
  139.8 3.9 subtract_bitcast_fusion.11
  143.7 2.6 fusion.80
  148.9 2.6 subtract_bitcast_fusion.10
  152.8 2.8 add_bitcast_fusion.10
  157.1 5.2 copy.372
  162.4 5.0 all-to-all-start.1
  171.0 90.0 %all-reduce.3.cloned.1.call-done = (f32[1,256,1024]{2,1,0:T(8,128)}, f32[1,256,1024]{2,1,0:T(8,128)}) async-done(((f32[1,256,1024]{2,1,0:T(8,128)}, f32[1,256,1024]{2,1,0:T(8,128)}), (f32[1,256,1024]{2,1,0:T(8,128)}, f32[1,256,1024]{2,1,0:T(8,128)})) %all-reduce.3.cloned.1.call-update) | async-done | bytes 2097168 | tf_op jit(solution)/shard_map/psum | solution.py:18
  260.9 4.7 fusion.192
  268.6 5.0 copy.373
  273.6 5.3 copy.374
  278.9 4.6 fusion.663
  285.6 3.2 fusion.318
  301.9 2.8 subtract_bitcast_fusion.8
  312.5 2.9 copy.386
  315.4 4.8 fusion.314
  320.2 3.1 copy.385
  323.3 3.6 fusion.316
  343.5 3.2 copy.395
  346.8 50.7 %all_to_all.72 = f32[2,2,1,256,1024]{3,0,2,1,4:T(2,128)S(1)} all-to-all(f32[2,2,1,256,1024]{3,0,2,1,4:T(2,128)S(1)} %copy.395), channel_id=1, replica_groups=mesh['shot'=2,'row'=4,'freq'=4] {'row'}, dimensions={4} | all-to-all | bytes 8388608 | tf_op jit(solution)/shard_map/all_to_all | solution.py:129
  397.5 2.7 copy.396
  400.3 5.7 copy.397
  408.5 2.9 fusion.56
  411.4 2.9 fusion.54
  414.3 2.9 fusion.130
  417.2 3.6 subtract_bitcast_fusion.5
  426.0 2.6 subtract_bitcast_fusion.4
  429.8 2.6 add_bitcast_fusion.4
  434.6 2.9 fusion.40
  437.5 2.9 fusion.38
  440.3 3.0 fusion.136
  443.4 4.0 subtract_bitcast_fusion.3
  447.4 2.6 fusion.32
  452.5 2.6 subtract_bitcast_fusion.2
  456.4 2.8 add_bitcast_fusion.2
  460.8 5.2 copy.418
  466.0 4.9 all-to-all-start.3
  471.0 2.6 copy.436
  474.9 5.7 cosine_bitcast_fusion
  484.7 4.7 fusion.10
  490.7 28.5 %all-to-all-done.3 = f32[2,2,1,1024,256]{4,0,2,1,3:T(2,128)} async-done(((f32[2,2,1,1024,256]{4,0,2,1,3:T(2,128)}), f32[2,2,1,1024,256]{4,0,2,1,3:T(2,128)}, u32[]{:S(2)}, u32[]{:S(2)}) %all-to-all-start.3) | async-done | bytes 4194336 | tf_op jit(solution)/shard_map/all_to_all | solution.py:134
  519.2 5.0 copy.419
  524.2 5.3 copy.420
  529.4 4.6 fusion.661
  536.1 3.2 fusion.306
  562.1 3.0 pad_maximum_fusion.6
  565.1 3.0 copy.444
  568.1 4.3 fusion.14
  574.3 13.1 %reduce-scatter.5.cloned.1.call-done = f32[256,256]{0,1:T(8,128)} async-done(((f32[256,1024]{0,1:T(8,128)}), f32[256,256]{0,1:T(8,128)}) %reduce-scatter.5.cloned.1.call-update) | async-done | bytes 262160 | tf_op jit(solution)/shard_map/reduce_scatter | solution.py:138
  (137 shorter events, 135.5 us)
Async XLA Ops:
  8.9 1.6 copy-start.19
  38.1 53.7 %all-to-all-start = ((f32[2,2,1,256,1024]{3,0,2,1,4:T(2,128)}), f32[2,2,1,256,1024]{3,0,2,1,4:T(2,128)}, u32[]{:S(2)}, u32[]{:S(2)}) async-start(f32[2,2,1,256,1024]{3,0,2,1,4:T(2,128)} %copy.346), calls=%async_computation | async-start | bytes 8388608 | tf_op jit(solution)/shard_map/all_to_all | solution.py:129
  48.1 82.2 %copy-start.8 = (f32[8,128,256]{2,1,0:T(8,128)}, f32[8,128,256]{2,1,0:T(8,128)S(1)}, u32[]{:S(2)}) copy-start(f32[8,128,256]{2,1,0:T(8,128)S(1)} %get-tuple-element.67) | copy-start | bytes 3145732
  162.4 5.1 copy-start.21
  162.4 7.0 %copy-start.20 = (f32[1,256,1024]{2,1,0:T(8,128)S(1)}, f32[1,256,1024]{2,1,0:T(8,128)}, u32[]{:S(2)}) copy-start(f32[1,256,1024]{2,1,0:T(8,128)} %param.7) | copy-start | bytes 3145732
  162.4 106.2 %all-to-all-start.1 = ((f32[2,2,1,1024,256]{4,0,2,1,3:T(2,128)}), f32[2,2,1,1024,256]{4,0,2,1,3:T(2,128)}, u32[]{:S(2)}, u32[]{:S(2)}) async-start(f32[2,2,1,1024,256]{4,0,2,1,3:T(2,128)} %copy.372), calls=%async_computation.1 | async-start | bytes 8388608 | tf_op jit(solution)/shard_map/all_to_all | solution.py:134
  167.4 93.5 %all-reduce.3.cloned.1.call-start = ((), (), s32[]{:S(2)}) async-start(), calls=%async_computation.8 | async-start | bytes 4194304 | tf_op jit(solution)/shard_map/psum | solution.py:18
  265.7 2.9 copy-start.11
  265.7 2.9 copy-start.13
  285.6 3.2 copy-start.6
  291.1 1.9 copy-start.14
  293.0 2.0 copy-start.7
  307.1 1.3 copy-start.1
  308.4 1.2 copy-start.17
  308.4 1.5 copy-start.18
  323.2 3.6 copy-start.2
  323.3 3.6 copy-start.15
  326.9 2.0 copy-start.5
  432.6 1.2 copy-start.9
  466.0 53.1 %all-to-all-start.3 = ((f32[2,2,1,1024,256]{4,0,2,1,3:T(2,128)}), f32[2,2,1,1024,256]{4,0,2,1,3:T(2,128)}, u32[]{:S(2)}, u32[]{:S(2)}) async-start(f32[2,2,1,1024,256]{4,0,2,1,3:T(2,128)} %copy.418), calls=%async_computation.3 | async-start | bytes 8388608 | tf_op jit(solution)/shard_map/all_to_all | solution.py:134
  470.9 2.7 copy-start.12
  470.9 103.4 %reduce-scatter.3.cloned.1.call-start = ((), (), s32[]{:S(2)}) async-start(), calls=%async_computation.6 | async-start | bytes 1310720 | tf_op jit(solution)/shard_map/reduce_scatter | solution.py:138
  490.7 96.8 %reduce-scatter.5.cloned.1.call-start = ((), (), s32[]{:S(2)}) async-start(), calls=%async_computation.7 | async-start | bytes 1310720 | tf_op jit(solution)/shard_map/reduce_scatter | solution.py:138
  536.1 3.2 copy-start.3
  541.8 1.9 copy-start.16
  543.7 2.0 copy-start.4
  555.2 2.3 copy-start.10
  557.5 2.5 copy-start
Sparse Core Ops, SparseCore 0:
  171.2 89.6 all-reduce.2
  490.8 26.5 reduce-scatter.2
  562.2 25.1 reduce-scatter.4
where the time goes:
time: 606 us; the launch traced here: 596 us
  waiting for transfers between devices  175 us (29%)
  matrix products  170 us (28%)
  local copies, waits for them, and re-layouts  125 us (21%)
  blocking collectives  50.7 us (8%)
  other arithmetic  42.9 us (7%)
  between operations  17.4 us (3%)
  starting transfers between devices  14.9 us (2%)
    dot_general x64, matrix products, contract(): return jnp.einsum(form, left, right, precision=lax.Precision.HIGHEST)  170 us
    psum x1, waiting for transfers between devices, spread(): return lax.psum(kept, axis)  90 us
    all_to_all x1, blocking collectives, body(): lax.all_to_all(fields, 'row', split_axis=4, concat_axis=3, tiled=True)  50.7 us
    all_to_all x1, waiting for transfers between devices, body(): lax.all_to_all(fields, 'row', split_axis=4, concat_axis=3, tiled=True)  43.7 us
    all_to_all x2, waiting for transfers between devices, body(): lax.all_to_all(fields, 'row', split_axis=3, concat_axis=4, tiled=True)  28.5 us
    all_to_all x4, local copies, waits for them, and re-layouts, body(): lax.all_to_all(fields, 'row', split_axis=3, concat_axis=4, tiled=True)  20.5 us
    another operation x4, local copies, waits for them, and re-layouts, transform(): return jnp.stack([out_re.reshape(shape), out_im.reshape(shape)], axis=1)  19.1 us
    all_to_all x4, local copies, waits for them, and re-layouts, body(): lax.all_to_all(fields, 'row', split_axis=4, concat_axis=3, tiled=True)  18.9 us
  transfers between devices with their start and end apart: 6, of which 4 were waited for; matrix products, arithmetic and copies ran while one was open for 15% of the time, Pallas kernels for 0%

commit v1 on v0

--- a/solution.py
+++ b/solution.py
@@ -131,7 +131,19 @@
         items = transform(items, -1.0, False)
         items = shift_phase(items, omega, kx_all, ky_own, total)
         fields = transform(items, 1.0, False)
-        fields = lax.all_to_all(fields, "row", split_axis=3, concat_axis=4, tiled=True)
+        ways, here = (lax.axis_size("row"), lax.axis_index("row"))
+        width_2 = fields.shape[3] // ways
+        dims = list(fields.shape)
+        dims[3] = width_2
+        height_2 = dims[4]
+        dims[4] = height_2 * ways
+        full = jnp.zeros(dims, fields.dtype)
+        for mask in range(ways):
+            part = lax.dynamic_slice_in_dim(fields, (here ^ mask) * width_2, width_2, axis=3)
+            if mask:
+                part = lax.ppermute(part, "row", [(d, d ^ mask) for d in range(ways)])
+            full = lax.dynamic_update_slice_in_dim(full, part, (here ^ mask) * height_2, axis=4)
+        fields = full
         fields = transform(fields, 1.0, True)
         fields = correct(fields, slab, omega)
         images.append(image_term(fields))

time: 606 us -> 514 us (0.85)
  waiting for transfers between devices: 175 us -> 112 us
  local copies, waits for them, and re-layouts: 125 us -> 103 us
    psum x1, waiting for transfers between devices: 90 us -> 0.01 us  [spread(): return lax.psum(kept, axis)]
    ppermute x0 -> x6, waiting for transfers between devices: none -> 56.3 us  [body(): part = lax.ppermute(part, 'row', [(d, d ^ mask) for d in range(ways)])]
    all_to_all x2 -> x0, waiting for transfers between devices: 28.5 us -> none  [body(): lax.all_to_all(fields, 'row', split_axis=3, concat_axis=4, tiled=True)]
    all_to_all x4 -> x0, local copies, waits for them, and re-layouts: 20.5 us -> none  [body(): lax.all_to_all(fields, 'row', split_axis=3, concat_axis=4, tiled=True)]
    dynamic_update_slice x0 -> x6, local copies, waits for them, and re-layouts: none -> 14.2 us  [body(): lax.dynamic_update_slice_in_dim(full, part, (here ^ mask) * height_2, axi...]
    another operation x4 -> x2, local copies, waits for them, and re-layouts: 19.1 us -> 8.67 us  [transform(): return jnp.stack([out_re.reshape(shape), out_im.reshape(shape)], axis=1)]
    all_to_all x2 -> x0, starting transfers between devices: 9.89 us -> none  [body(): lax.all_to_all(fields, 'row', split_axis=3, concat_axis=4, tiled=True)]
    slice x2 -> x0, local copies, waits for them, and re-layouts: 9.2 us -> none  [transform(): imag_part = block[:, 1].reshape((count * freqs,) + plane)]
  transfers between devices with their start and end apart: 6 -> 10, of which waited for: 4 -> 6; matrix products, arithmetic and copies ran while one was open for 15% -> 30% of each run, Pallas kernels for 0% -> 0%
where the time goes in v1:
time: 514 us; the launch traced here: 505 us
  matrix products  167 us (32%)
  waiting for transfers between devices  112 us (22%)
  local copies, waits for them, and re-layouts  103 us (20%)
  blocking collectives  50.7 us (10%)
  other arithmetic  45.6 us (9%)
  between operations  17.6 us (3%)
  starting transfers between devices  9.04 us (2%)
    dot_general x64, matrix products, contract(): return jnp.einsum(form, left, right, precision=lax.Precision.HIGHEST)  167 us
    ppermute x6, waiting for transfers between devices, body(): part = lax.ppermute(part, 'row', [(d, d ^ mask) for d in range(ways)])  56.3 us
    all_to_all x1, blocking collectives, body(): lax.all_to_all(fields, 'row', split_axis=4, concat_axis=3, tiled=True)  50.7 us
    all_to_all x1, waiting for transfers between devices, body(): lax.all_to_all(fields, 'row', split_axis=4, concat_axis=3, tiled=True)  40.1 us
    all_to_all x4, local copies, waits for them, and re-layouts, body(): lax.all_to_all(fields, 'row', split_axis=4, concat_axis=3, tiled=True)  19.1 us
    reduce_scatter x2, waiting for transfers between devices, body(): lax.psum_scatter(term, 'freq', scatter_dimension=1, tiled=True)  15.8 us
    dynamic_update_slice x6, local copies, waits for them, and re-layouts, body(): lax.dynamic_update_slice_in_dim(full, part, (here ^ mask) * height_2, axi...  14.2 us
    sub x5, other arithmetic, rotate(): real_part * cos_v - imag_part * sin_v  13 us
  transfers between devices with their start and end apart: 10, of which 6 were waited for; matrix products, arithmetic and copies ran while one was open for 30% of the time, Pallas kernels for 0%

profile of v1, /device:TPU:0, one launch (start us, length us, event | category | flops | bytes accessed | tf_op | source)
XLA Modules:
  0.0 504.8 jit_solution(6449799745272319637)
XLA Ops:
  32.4 5.4 %copy.234 = f32[2,2,1,256,1024]{3,0,2,1,4:T(2,128)} copy(f32[2,2,1,256,1024]{3,4,0,2,1:T(8,128)S(1)} %pad_maximum_fusion) | data formatting | bytes 8388608 | tf_op jit(solution)/shard_map/stack | solution.py:72
  37.8 5.0 all-to-all-start
  47.4 4.0 fusion.214
  51.5 40.1 %all-to-all-done = f32[2,2,1,256,1024]{3,0,2,1,4:T(2,128)} async-done(((f32[2,2,1,256,1024]{3,0,2,1,4:T(2,128)}), f32[2,2,1,256,1024]{3,0,2,1,4:T(2,128)}, u32[]{:S(2)}, u32[]{:S(2)}) %all-to-all-start) | async-done | bytes 4194336 | tf_op jit(solution)/shard_map/all_to_all | solution.py:129
  91.6 5.0 copy.235
  96.6 5.7 %copy.236 = f32[2,2,1,4,256,256]{5,4,3,1,0,2:T(8,128)} copy(f32[2,2,1,4,256,256]{4,5,3,1,0,2:T(8,128)} %bitcast.509) | data formatting | bytes 8388608 | tf_op jit(solution)/shard_map/all_to_all | solution.py:129
  102.4 2.5 fusion.666
  104.9 2.9 fusion.120
  107.8 2.9 fusion.118
  110.7 2.9 fusion.134
  113.6 3.6 subtract_bitcast_fusion.13
  117.2 2.6 fusion.112
  119.8 2.6 fusion.110
  122.4 2.6 subtract_bitcast_fusion.12
  126.2 2.6 add_bitcast_fusion.12
  131.0 2.9 fusion.104
  133.9 2.9 fusion.102
  136.8 3.0 fusion.140
  139.8 4.0 subtract_bitcast_fusion.11
  143.8 2.6 fusion.94
  146.4 2.6 add_bitcast_fusion.10
  150.2 2.6 fusion.96
  152.8 2.8 subtract_bitcast_fusion.10
  156.9 2.5 broadcast.572.clone
  163.4 4.7 fusion.230
  173.4 14.4 %collective-permute-done.1 = f32[2,2,1,256,256]{4,3,0,2,1:T(8,128)} collective-permute-done((f32[2,2,1,256,256]{4,3,0,2,1:T(8,128)}, f32[2,2,1,256,256]{4,3,0,2,1:T(8,128)}, u32[]{:S(2)}, u32[]{:S(2)}) %collective-permute-start.1) | collective-permute-done | bytes 1048608 | tf_op jit(solution)/shard_map/ppermute | solution.py:144
  190.2 19.3 %collective-permute-done.2 = f32[2,2,1,256,256]{4,3,0,2,1:T(8,128)} collective-permute-done((f32[2,2,1,256,256]{4,3,0,2,1:T(8,128)}, f32[2,2,1,256,256]{4,3,0,2,1:T(8,128)}, u32[]{:S(2)}, u32[]{:S(2)}) %collective-permute-start.2) | collective-permute-done | bytes 1048608 | tf_op jit(solution)/shard_map/ppermute | solution.py:144
  223.6 2.7 fusion.88
  236.0 2.5 fusion.35
  238.6 2.9 copy.269
  241.5 4.8 fusion.382
  246.2 3.1 copy.268
  249.4 3.6 fusion.384
  269.7 3.2 copy.278
  272.9 50.7 %all_to_all.36 = f32[2,2,1,256,1024]{3,0,2,1,4:T(2,128)S(1)} all-to-all(f32[2,2,1,256,1024]{3,0,2,1,4:T(2,128)S(1)} %copy.278), channel_id=1, replica_groups=mesh['shot'=2,'row'=4,'freq'=4] {'row'}, dimensions={4} | all-to-all | bytes 8388608 | tf_op jit(solution)/shard_map/all_to_all | solution.py:129
  323.7 2.8 copy.279
  326.4 5.6 %copy.280 = f32[2,2,1,4,256,256]{5,4,3,1,0,2:T(8,128)} copy(f32[2,2,1,4,256,256]{4,5,3,1,0,2:T(8,128)} %bitcast.510) | data formatting | bytes 8388608 | tf_op jit(solution)/shard_map/all_to_all | solution.py:129
  332.0 2.5 fusion.664
  334.6 2.9 fusion.72
  337.5 2.9 fusion.70
  340.3 2.9 fusion.146
  343.2 3.6 subtract_bitcast_fusion.5
  346.9 2.6 fusion.64
  349.4 2.6 fusion.62
  352.0 2.6 subtract_bitcast_fusion.4
  355.8 2.6 add_bitcast_fusion.4
  360.6 2.9 fusion.56
  363.5 2.9 fusion.54
  366.4 3.0 fusion.152
  369.4 3.9 subtract_bitcast_fusion.3
  373.4 2.6 fusion.46
  375.9 2.6 fusion.48
  378.5 2.7 add_bitcast_fusion.2
  382.5 2.8 subtract_bitcast_fusion.2
  386.4 2.5 broadcast.572
  391.5 4.6 cosine_bitcast_fusion
  401.5 2.6 copy.308
  405.6 4.7 fusion.26
  414.1 3.3 collective-permute-done.4
  419.8 19.3 %collective-permute-done.5 = f32[2,2,1,256,256]{4,3,0,2,1:T(8,128)} collective-permute-done((f32[2,2,1,256,256]{4,3,0,2,1:T(8,128)}, f32[2,2,1,256,256]{4,3,0,2,1:T(8,128)}, u32[]{:S(2)}, u32[]{:S(2)}) %collective-permute-start.5) | collective-permute-done | bytes 1048608 | tf_op jit(solution)/shard_map/ppermute | solution.py:144
  467.2 3.0 pad_maximum_fusion.4
  470.3 3.2 copy.322
  473.4 4.5 fusion.30
  479.8 15.8 %reduce-scatter.5.cloned.1.call-done = f32[256,256]{0,1:T(8,128)} async-done(((f32[256,1024]{0,1:T(8,128)}), f32[256,256]{0,1:T(8,128)}) %reduce-scatter.5.cloned.1.call-update) | async-done | bytes 262160 | tf_op jit(solution)/shard_map/reduce_scatter | solution.py:150
  (137 shorter events, 138.4 us)
Async XLA Ops:
  9.0 1.6 copy-start.13
  37.8 5.0 %copy-start.16 = (s32[4]{0:T(128)S(1)}, s32[4]{0:T(128)}, u32[]{:S(2)}) copy-start(s32[4]{0:T(128)} %param.8) | copy-start | bytes 52
  37.8 6.9 %copy-start.14 = (f32[1,256,1024]{2,1,0:T(8,128)S(1)}, f32[1,256,1024]{2,1,0:T(8,128)}, u32[]{:S(2)}) copy-start(f32[1,256,1024]{2,1,0:T(8,128)} %param.7) | copy-start | bytes 3145732
  37.8 53.8 %all-to-all-start = ((f32[2,2,1,256,1024]{3,0,2,1,4:T(2,128)}), f32[2,2,1,256,1024]{3,0,2,1,4:T(2,128)}, u32[]{:S(2)}, u32[]{:S(2)}) async-start(f32[2,2,1,256,1024]{3,0,2,1,4:T(2,128)} %copy.234), calls=%async_computation | async-start | bytes 8388608 | tf_op jit(solution)/shard_map/all_to_all | solution.py:129
  42.8 120.6 %all-reduce.3.cloned.1.call-start = ((), (), s32[]{:S(2)}) async-start(), calls=%async_computation.6 | async-start | bytes 4194304 | tf_op jit(solution)/shard_map/psum | solution.py:18
  46.3 433.5 %reduce-scatter.3.cloned.1.call-start = ((), (), s32[]{:S(2)}) async-start(), calls=%async_computation.4 | async-start | bytes 1310720 | tf_op jit(solution)/shard_map/reduce_scatter | solution.py:150
  51.5 78.8 %copy-start.4 = (f32[8,128,256]{2,1,0:T(8,128)}, f32[8,128,256]{2,1,0:T(8,128)S(1)}, u32[]{:S(2)}) copy-start(f32[8,128,256]{2,1,0:T(8,128)S(1)} %get-tuple-element.72) | copy-start | bytes 3145732
  161.6 9.5 %collective-permute-start = (f32[2,2,1,256,256]{4,3,0,2,1:T(8,128)}, f32[2,2,1,256,256]{4,3,0,2,1:T(8,128)}, u32[]{:S(2)}, u32[]{:S(2)}) collective-permute-start(f32[2,2,1,256,256]{4,3,0,2,1:T(8,128)} %get-tuple-element.54), channel_id=1, source_target_pairs={{0,4},{4,0},{8,12},{12,8},{1,5},{5,1},{9,13},{13,9},{2,6},{6,2},{1... | collective-permute-start | bytes 3145736 | tf_op jit(solution)/shard_map/ppermute | solution.py:144
  161.6 26.3 %collective-permute-start.1 = (f32[2,2,1,256,256]{4,3,0,2,1:T(8,128)}, f32[2,2,1,256,256]{4,3,0,2,1:T(8,128)}, u32[]{:S(2)}, u32[]{:S(2)}) collective-permute-start(f32[2,2,1,256,256]{4,3,0,2,1:T(8,128)} %get-tuple-element.55), channel_id=1, source_target_pairs={{0,8},{4,12},{8,0},{12,4},{1,9},{5,13},{9,1},{13,5},{2,10},{6,14},... | collective-permute-start | bytes 3145736 | tf_op jit(solution)/shard_map/ppermute | solution.py:144
  161.6 48.0 %collective-permute-start.2 = (f32[2,2,1,256,256]{4,3,0,2,1:T(8,128)}, f32[2,2,1,256,256]{4,3,0,2,1:T(8,128)}, u32[]{:S(2)}, u32[]{:S(2)}) collective-permute-start(f32[2,2,1,256,256]{4,3,0,2,1:T(8,128)} %get-tuple-element.52), channel_id=1, source_target_pairs={{0,12},{4,8},{8,4},{12,0},{1,13},{5,9},{9,5},{13,1},{2,14},{6,10},... | collective-permute-start | bytes 3145736 | tf_op jit(solution)/shard_map/ppermute | solution.py:144
  168.2 2.9 copy-start.7
  168.2 2.9 copy-start.9
  233.2 1.3 copy-start.1
  234.5 1.2 copy-start.11
  234.5 1.5 copy-start.12
  249.4 3.6 copy-start.2
  249.4 3.6 copy-start.10
  253.0 2.0 copy-start.3
  358.7 1.2 copy-start.5
  389.0 2.5 copy-start.15
  391.1 20.6 %collective-permute-start.3 = (f32[2,2,1,256,256]{4,3,0,2,1:T(8,128)}, f32[2,2,1,256,256]{4,3,0,2,1:T(8,128)}, u32[]{:S(2)}, u32[]{:S(2)}) collective-permute-start(f32[2,2,1,256,256]{4,3,0,2,1:T(8,128)} %get-tuple-element.46), channel_id=1, source_target_pairs={{0,4},{4,0},{8,12},{12,8},{1,5},{5,1},{9,13},{13,9},{2,6},{6,2},{1... | collective-permute-start | bytes 3145736 | tf_op jit(solution)/shard_map/ppermute | solution.py:144
  391.1 26.3 %collective-permute-start.4 = (f32[2,2,1,256,256]{4,3,0,2,1:T(8,128)}, f32[2,2,1,256,256]{4,3,0,2,1:T(8,128)}, u32[]{:S(2)}, u32[]{:S(2)}) collective-permute-start(f32[2,2,1,256,256]{4,3,0,2,1:T(8,128)} %get-tuple-element.47), channel_id=1, source_target_pairs={{0,8},{4,12},{8,0},{12,4},{1,9},{5,13},{9,1},{13,5},{2,10},{6,14},... | collective-permute-start | bytes 3145736 | tf_op jit(solution)/shard_map/ppermute | solution.py:144
  391.5 7.1 %copy-start.8 = (f32[1,256,1024]{2,1,0:T(8,128)S(1)}, f32[1,256,1024]{2,1,0:T(8,128)}, u32[]{:S(2)}) copy-start(f32[1,256,1024]{2,1,0:T(8,128)} %copy-done.7) | copy-start | bytes 3145732
  404.1 35.0 %collective-permute-start.5 = (f32[2,2,1,256,256]{4,3,0,2,1:T(8,128)}, f32[2,2,1,256,256]{4,3,0,2,1:T(8,128)}, u32[]{:S(2)}, u32[]{:S(2)}) collective-permute-start(f32[2,2,1,256,256]{4,3,0,2,1:T(8,128)} %get-tuple-element.44), channel_id=1, source_target_pairs={{0,12},{4,8},{8,4},{12,0},{1,13},{5,9},{9,5},{13,1},{2,14},{6,10},... | collective-permute-start | bytes 3145736 | tf_op jit(solution)/shard_map/ppermute | solution.py:144
  411.5 84.2 %reduce-scatter.5.cloned.1.call-start = ((), (), s32[]{:S(2)}) async-start(), calls=%async_computation.5 | async-start | bytes 1310720 | tf_op jit(solution)/shard_map/reduce_scatter | solution.py:150
  460.3 2.4 copy-start.6
  462.7 2.5 copy-start
Sparse Core Ops, SparseCore 0:
  46.6 90.1 all-reduce.2
  411.6 28.3 reduce-scatter.2
  467.3 28.2 reduce-scatter.4
